TPU v7x, 32 devices: a whole 2x2x4 slice. The times are simulated.
32 devices in a mesh: slab: 16 (over z, y, x), feat: 2 (over core).
Axes of the slice: x: 2, y: 2, z: 4, core: 2. Of those that a mesh axis runs over, the one named last changes fastest.
Arguments:
- states: float32 [40, 8192], P(None, ('slab', 'feat')), may hold values from -6 to 6
- inputs: float32 [8192], P(('slab', 'feat')), may hold values from -4 to 4
- targets: float32 [40, 8192], P(None, ('slab', 'feat')), may hold values from -4 to 4
Outputs:
- local_operators: float32 [16, 40, 862], P('slab', 'feat')
- scaled_duals: float32 [16, 40, 862], P('slab', 'feat')
- consensus: float32 [40, 862], P('feat')
- residual_history: float32 [2, 2], replicated
All inputs are finite; a program needn't handle non-finite values.
Results may differ from a plain program's by a relative error of at most 0.0003.
Values sent between devices are 32-bit elements; how exact they have to be, the bound alone decides.
A program may use at most 64 MiB of HBM per device.

v0:
```python
import jax
import jax.numpy as jnp
from jax import lax
from jax.sharding import PartitionSpec as P

ITERS = 2


penalty = 1.0


def features(states, inputs):
    reduced = states.shape[0]
    blocks = [states]
    for column in range(reduced):
        blocks.append(states[column : column + 1] * states[column:])
    blocks.append(inputs[None, :])
    blocks.append(jnp.ones_like(inputs)[None, :])
    return jnp.concatenate(blocks, 0)


def product(left, right):
    return jnp.dot(left, right, precision=lax.Precision.HIGHEST, preferred_element_type=jnp.float32)


def solve_rows(factor, right_side):
    return jax.scipy.linalg.cho_solve((factor, True), right_side.T).T


def slab_average(summand):
    return lax.psum(summand, "slab")


def shards(states, inputs, targets):
    reduced = states.shape[0]
    feat_count = lax.axis_size("feat")
    slab_count = lax.axis_size("slab")
    half_rows = reduced // feat_count
    all_states, all_targets, all_inputs = (
        lax.all_gather(states, "feat", axis=1, tiled=True),
        lax.all_gather(targets, "feat", axis=1, tiled=True),
        lax.all_gather(inputs, "feat", axis=0, tiled=True),
    )
    design = features(all_states, all_inputs)
    row_total = design.shape[1]
    gram_matrix = product(design, design.T) / row_total
    first_row = lax.axis_index("feat") * half_rows
    picked = lax.dynamic_slice_in_dim(all_targets, first_row, half_rows, 0)
    cross = product(picked, design.T) / row_total
    width = gram_matrix.shape[0]
    factor = jnp.linalg.cholesky(gram_matrix + penalty * jnp.eye(width, dtype=jnp.float32))
    consensus = jnp.zeros((half_rows, width), jnp.float32)
    duals = jnp.zeros((half_rows, width), jnp.float32)
    operator_rows = duals
    primal_list = []
    dual_list = []
    for sweep in range(ITERS):
        operator_rows = solve_rows(factor, cross + penalty * (consensus - duals))
        updated = slab_average(operator_rows + duals) / slab_count
        duals = duals + operator_rows - updated
        primal_part = jnp.sum(jnp.square(operator_rows - updated))
        dual_part = penalty * penalty * jnp.sum(jnp.square(updated - consensus))
        primal_sum, dual_sum = lax.psum((primal_part, dual_part), ("slab", "feat"))
        primal_list.append(primal_sum)
        dual_list.append(dual_sum)
        consensus = updated
    history = jnp.stack([jnp.stack(primal_list), jnp.stack(dual_list)])
    residual_history = jnp.sqrt(history / (slab_count * reduced * width))
    return (operator_rows[None], duals[None], consensus, residual_history)


def solution(mesh):
    in_specs = (P(None, ("slab", "feat")), P(("slab", "feat")), P(None, ("slab", "feat")))
    out_specs = (P("slab", "feat", None), P("slab", "feat", None), P("feat", None), P())
    return jax.shard_map(shards, mesh=mesh, in_specs=in_specs, out_specs=out_specs, check_vma=False)
```

profile of v0, /device:TPU:0, one launch (start us, length us, event | category | flops | bytes accessed | tf_op | source)
XLA Modules:
  0.0 593.1 jit_solution(18076487294671778881)
XLA Ops:
  7.2 2.2 all_gather.9
  18.4 1.9 all-gather
  20.3 2.0 all_gather.11
  22.9 11.9 %concatenate.45 = f32[862,512]{1,0:T(8,128)S(1)} concatenate(f32[40,512]{1,0:T(8,128)S(1)} %all_gather.9, f32[40,512]{1,0:T(8,128)S(1)} %broadcast_multiply_fusion.1, f32[39,512]{1,0:T(8,128)S(1)} %slice_multiply_fusion.6, f32[38,512]{1,0:T(8,128)S(1)} %slice_multiply_fusion.5, f32[37,512]{1,0:T(8,128)S(1)} %slice_multiply_fusion.4, f32[36,512]{1,0:T(8,128)S(1)} %slice_multiply_fusion.3, ...), dimensions={0} | concatenate | bytes 3530752 | tf_op jit(solution)/shard_map/concatenate | solution.py:19
  34.8 7.8 %convert_add_fusion = (f32[862,862]{0,1:T(8,128)}, f32[862,862]{0,1:T(8,128)}) fusion(f32[862,512]{1,0:T(8,128)S(1)} %concatenate.45), kind=kOutput, calls=%fused_computation.8 | convolution fusion | flops 4568234496 | bytes 7709728 | tf_op jit(solution)/shard_map/dot_general | solution.py:23
  42.6 3.6 copy.12
  46.3 2.3 fusion.1
  48.5 1.6 copy-done.3
  50.2 11.7 %cholesky.196 = f32[128,128]{1,0:T(8,128)S(1)} custom-call(f32[128,128]{1,0:T(8,128)S(1)} %cholesky.508), custom_call_target="Cholesky" | custom-call | tf_op jit(solution)/shard_map/jit(cholesky)/cholesky | solution.py:51
  62.1 9.8 %custom-call.56 = f32[1,128,128]{1,2,0:T(8,128)S(1)} custom-call(f32[1,128,128]{2,1,0:T(8,128)S(1)} %get-tuple-element.104), custom_call_target="InvertDiagBlocksLowerTriangular" | custom-call | tf_op jit(solution)/shard_map/jit(cholesky)/cholesky | solution.py:51
  72.0 1.4 constant_dynamic-update-slice_fusion.62
  73.4 1.5 convolution_subtract_fusion
  75.5 12.5 %cholesky.217 = f32[128,128]{1,0:T(8,128)S(1)} custom-call(f32[128,128]{1,0:T(8,128)} %cholesky.512), custom_call_target="Cholesky" | custom-call | tf_op jit(solution)/shard_map/jit(cholesky)/cholesky | solution.py:51
  88.7 11.0 %custom-call.57 = f32[1,128,128]{1,2,0:T(8,128)S(1)} custom-call(f32[1,128,128]{2,1,0:T(8,128)} %get-tuple-element.101), custom_call_target="InvertDiagBlocksLowerTriangular" | custom-call | tf_op jit(solution)/shard_map/jit(cholesky)/cholesky | solution.py:51
  100.1 1.6 convolution_subtract_fusion.1
  101.8 11.7 %cholesky.413 = f32[128,128]{1,0:T(8,128)S(1)} custom-call(f32[128,128]{1,0:T(8,128)S(1)} %cholesky.517), custom_call_target="Cholesky" | custom-call | tf_op jit(solution)/shard_map/jit(cholesky)/cholesky | solution.py:51
  113.5 9.8 %custom-call.58 = f32[1,128,128]{1,2,0:T(8,128)S(1)} custom-call(f32[1,128,128]{2,1,0:T(8,128)S(1)} %get-tuple-element.98), custom_call_target="InvertDiagBlocksLowerTriangular" | custom-call | tf_op jit(solution)/shard_map/jit(cholesky)/cholesky | solution.py:51
  123.7 1.7 convolution_subtract_fusion.2
  125.4 11.9 %cholesky.432 = f32[128,128]{1,0:T(8,128)S(1)} custom-call(f32[128,128]{1,0:T(8,128)S(1)} %cholesky.522), custom_call_target="Cholesky" | custom-call | tf_op jit(solution)/shard_map/jit(cholesky)/cholesky | solution.py:51
  137.3 9.8 %custom-call.59 = f32[1,128,128]{1,2,0:T(8,128)S(1)} custom-call(f32[1,128,128]{2,1,0:T(8,128)S(1)} %get-tuple-element.95), custom_call_target="InvertDiagBlocksLowerTriangular" | custom-call | tf_op jit(solution)/shard_map/jit(cholesky)/cholesky | solution.py:51
  147.4 1.7 convolution_subtract_fusion.3
  149.1 11.7 %cholesky.451 = f32[128,128]{1,0:T(8,128)S(1)} custom-call(f32[128,128]{1,0:T(8,128)S(1)} %cholesky.527), custom_call_target="Cholesky" | custom-call | tf_op jit(solution)/shard_map/jit(cholesky)/cholesky | solution.py:51
  160.9 9.8 %custom-call.60 = f32[1,128,128]{1,2,0:T(8,128)S(1)} custom-call(f32[1,128,128]{2,1,0:T(8,128)S(1)} %get-tuple-element.92), custom_call_target="InvertDiagBlocksLowerTriangular" | custom-call | tf_op jit(solution)/shard_map/jit(cholesky)/cholesky | solution.py:51
  170.9 1.5 convolution_subtract_fusion.4
  172.5 11.9 %cholesky.471 = f32[128,128]{1,0:T(8,128)S(1)} custom-call(f32[128,128]{1,0:T(8,128)S(1)} %cholesky.532), custom_call_target="Cholesky" | custom-call | tf_op jit(solution)/shard_map/jit(cholesky)/cholesky | solution.py:51
  184.4 9.8 %custom-call.61 = f32[1,128,128]{1,2,0:T(8,128)S(1)} custom-call(f32[1,128,128]{2,1,0:T(8,128)S(1)} %get-tuple-element.89), custom_call_target="InvertDiagBlocksLowerTriangular" | custom-call | tf_op jit(solution)/shard_map/jit(cholesky)/cholesky | solution.py:51
  194.4 1.2 convolution_subtract_fusion.5
  195.6 8.6 %cholesky.492 = f32[94,94]{1,0:T(8,128)S(1)} custom-call(f32[94,94]{1,0:T(8,128)S(1)} %convolution_subtract_fusion.5), custom_call_target="Cholesky" | custom-call | tf_op jit(solution)/shard_map/jit(cholesky)/cholesky | solution.py:51
  213.7 1.0 copy-done.1
  214.6 17.4 %while.4 = (s32[]{:T(128)}, f32[862,862]{1,0:T(8,128)}, s32[6,2]{0,1:T(2,128)S(1)}, f32[6,128,128]{2,1,0:T(8,128)S(1)}, s32[]{:T(128)}) while((s32[]{:T(128)}, f32[862,862]{1,0:T(8,128)}, s32[6,2]{0,1:T(2,128)S(1)}, f32[6,128,128]{2,1,0:T(8,128)S(1)}, s32[]{:T(128)}) %tuple.120), condition=%wide.while_cond.clone, body=%wide.while_body.clone.sunk | while | flops 2 | bytes 131189 | solution.py:27
  215.2 2.3 bitcast_dynamic-update-slice_fusion.2
  218.1 2.3 bitcast_dynamic-update-slice_fusion.2
  221.1 2.3 bitcast_dynamic-update-slice_fusion.2
  224.0 2.3 bitcast_dynamic-update-slice_fusion.2
  226.9 2.3 bitcast_dynamic-update-slice_fusion.2
  229.8 2.3 bitcast_dynamic-update-slice_fusion.2
  232.1 1.0 fusion.39
  234.0 69.8 %custom-call.64 = f32[7,128,128]{1,2,0:T(8,128)S(1)} custom-call(f32[7,128,128]{2,1,0:T(8,128)} %pad_maximum_fusion), custom_call_target="InvertDiagBlocksLowerTriangular" | custom-call | tf_op jit(solution)/shard_map/jit(_cho_solve)/triangular_solve | solution.py:27
  303.8 3.1 convolution_multiply_fusion
  317.7 107.1 %all-reduce.7.cloned.1.call-done = f32[20,862]{1,0:T(8,128)} async-done(((f32[20,862]{1,0:T(8,128)}), f32[20,862]{1,0:T(8,128)}) %all-reduce.7.cloned.1.call-update) | async-done | bytes 68976 | tf_op jit(solution)/shard_map/psum | solution.py:31
  424.8 1.0 add_bitcast_fusion
  432.5 1.5 bitcast_add_fusion.1
  434.7 103.8 %all-reduce.9.cloned.1.call-done = f32[20,862]{1,0:T(8,128)} async-done(((f32[20,862]{1,0:T(8,128)}), f32[20,862]{1,0:T(8,128)}) %all-reduce.9.cloned.1.call-update) | async-done | bytes 68976 | tf_op jit(solution)/shard_map/psum | solution.py:31
  538.6 1.7 multiply_reduce_fusion.2
  540.3 0.9 subtract_bitcast_fusion
  541.9 40.7 %all-reduce.3 = (f32[1]{0:T(128)}, f32[1]{0:T(128)}, f32[1]{0:T(128)}, f32[1]{0:T(128)}) all-reduce(f32[1]{0:T(128)} %bitcast.80, f32[1]{0:T(128)} %bitcast.79, f32[1]{0:T(128)} %bitcast.77, f32[1]{0:T(128)} %bitcast.76), channel_id=1, replica_groups=mesh['slab'=16,'feat'=2] {'slab','feat'}, use_global_device_ids=true, to_apply=%region_23.25 | all-reduce | flops 4 | bytes 32 | tf_op jit(solution)/shard_map/psum | solution.py:63
  582.6 1.3 maximum_bitcast_fusion.1
  583.9 1.4 maximum_bitcast_fusion
  (199 shorter events, 40.8 us)
Async XLA Ops:
  7.2 11.2 %copy-start.10 = (f32[256]{0:T(256)S(1)}, f32[256]{0:T(256)}, u32[]{:S(2)}) copy-start(f32[256]{0:T(256)} %param.6) | copy-start | bytes 3076
  7.2 13.2 %copy-start.8 = (f32[40,256]{1,0:T(8,128)S(1)}, f32[40,256]{1,0:T(8,128)}, u32[]{:S(2)}) copy-start(f32[40,256]{1,0:T(8,128)} %param.7) | copy-start | bytes 122884
  7.2 417.6 %all-reduce.7.cloned.1.call-start = ((), (), s32[]{:S(2)}) async-start(), calls=%async_computation | async-start | bytes 172032 | tf_op jit(solution)/shard_map/psum | solution.py:31
  34.8 7.8 %copy-start = (f32[862,512]{1,0:T(8,128)}, f32[862,512]{1,0:T(8,128)S(1)}, u32[]{:S(2)}) copy-start(f32[862,512]{1,0:T(8,128)S(1)} %concatenate.45) | copy-start | bytes 5296132
  48.5 1.6 copy-start.3
  212.7 0.9 copy-start.9
  212.7 0.9 copy-start.11
  212.7 1.9 copy-start.6
  213.0 1.7 copy-start.1
  232.1 75.0 %copy-start.2 = (f32[862,862]{1,0:T(8,128)S(1)}, f32[862,862]{1,0:T(8,128)}, u32[]{:S(2)}) copy-start(f32[862,862]{1,0:T(8,128)} %get-tuple-element.201) | copy-start | bytes 8916532
  306.9 10.8 %copy-start.4 = (f32[20,862]{1,0:T(8,128)}, f32[20,862]{1,0:T(8,128)S(1)}, u32[]{:S(2)}) copy-start(f32[20,862]{1,0:T(8,128)S(1)} %convolution_multiply_fusion) | copy-start | bytes 206884
  317.7 220.9 %all-reduce.9.cloned.1.call-start = ((), (), s32[]{:S(2)}) async-start(), calls=%async_computation.1 | async-start | bytes 172032 | tf_op jit(solution)/shard_map/psum | solution.py:31
  424.8 7.6 %copy-start.5 = (f32[20,862]{1,0:T(8,128)S(1)}, f32[20,862]{1,0:T(8,128)}, u32[]{:S(2)}) copy-start(f32[20,862]{1,0:T(8,128)} %all-reduce.7.cloned.1.call-done) | copy-start | bytes 206884
  540.3 45.6 %copy-start.7 = (f32[20,862]{1,0:T(8,128)}, f32[20,862]{1,0:T(8,128)S(1)}, u32[]{:S(2)}) copy-start(f32[20,862]{1,0:T(8,128)S(1)} %get-tuple-element.45) | copy-start | bytes 206884
Sparse Core Ops, SparseCore 0:
  317.8 106.9 all-reduce.6
  434.1 104.3 all-reduce.8
where the time goes:
time: 600 us; the launch traced here: 593 us
  other arithmetic  236 us (39%)
  waiting for transfers between devices  211 us (35%)
  blocking collectives  46.8 us (8%)
  local copies, waits for them, and re-layouts  42.8 us (7%)
  matrix products  36.1 us (6%)
  between operations  20.1 us (3%)
    psum x2, waiting for transfers between devices, slab_average(): return lax.psum(summand, 'slab')  211 us
    another operation x26, other arithmetic, shards(): jnp.linalg.cholesky(gram_matrix + penalty * jnp.eye(width, dtype=jnp.floa...  145 us
    another operation x8, other arithmetic, solve_rows(): return jax.scipy.linalg.cho_solve((factor, True), right_side.T).T  73 us
    psum x1, blocking collectives, shards(): primal_sum, dual_sum = lax.psum((primal_part, dual_part), ('slab', 'feat'))  40.7 us
    another operation x26, local copies, waits for them, and re-layouts, solve_rows(): return jax.scipy.linalg.cho_solve((factor, True), right_side.T).T  18.6 us
    another operation x52, matrix products, solve_rows(): return jax.scipy.linalg.cho_solve((factor, True), right_side.T).T  13.1 us
    another operation x12, matrix products, shards(): jnp.linalg.cholesky(gram_matrix + penalty * jnp.eye(width, dtype=jnp.floa...  12.1 us
  transfers between devices with their start and end apart: 2, of which 2 were waited for; matrix products, arithmetic and copies ran while one was open for 0% of the time, Pallas kernels for 0%

commit v1 on v0

v1 whole, which is shorter than its diff:
```python
import functools

import jax
import jax.numpy as jnp
from jax import lax
from jax.experimental import pallas as pl
from jax.experimental.pallas import tpu as pltpu
from jax.sharding import PartitionSpec as P

penalty = 1.0
NN = (((1,), (0,)), ((), ()))
NT = (((1,), (1,)), ((), ()))


def exact(left, right, dims=NN):
    return lax.dot_general(left, right, dims, precision=lax.Precision.HIGHEST, preferred_element_type=jnp.float32)


def fast(left, right, dims=NN):
    return lax.dot_general(
        left.astype(jnp.bfloat16), right.astype(jnp.bfloat16), dims, preferred_element_type=jnp.float32
    )


def split(value):
    high = value.astype(jnp.bfloat16)
    return high, (value - high.astype(jnp.float32)).astype(jnp.bfloat16)


def triple(left, right):
    lh, ll = split(left)
    rh, rl = split(right)
    return fast(lh, rh) + (fast(lh, rl) + fast(ll, rh))


def eye_mask(size):
    return lax.broadcasted_iota(jnp.int32, (size, size), 0) == lax.broadcasted_iota(jnp.int32, (size, size), 1)


def refined_solve(right_side, system, inverse):
    answer = fast(right_side, inverse)
    for _ in range(3):
        answer = answer + fast(right_side - exact(answer, system), inverse)
    return answer


def invert_by_pivots(source, target):
    size = source.shape[0]
    target[...] = source[...]
    sub = lax.broadcasted_iota(jnp.int32, (size, 1), 0)
    lane = lax.broadcasted_iota(jnp.int32, (1, size), 1)

    def step(k, carry):
        row = target[pl.ds(k, 1), :]
        here = lane == k
        pivot = jnp.sum(jnp.where(here, row, 0.0), axis=1, keepdims=True)
        scaled = jnp.where(here, 1.0, row) / pivot
        whole = target[...]
        column = jnp.sum(jnp.where(here, whole, 0.0), axis=1, keepdims=True)
        column = jnp.where(sub == k, -1.0, column)
        kept = jnp.where(here | (sub == k), 0.0, whole)
        target[...] = kept - column * scaled
        return carry

    lax.fori_loop(0, size, step, 0)


def first_kernel(states, inputs, targets, local, system, inverse, phi, shifted):
    reduced, count = states.shape
    width = local.shape[1]
    row = 0
    phi[0:reduced, :] = states[...]
    row = reduced
    for i in range(reduced):
        phi[row : row + reduced - i, :] = states[i : i + 1, :] * states[i:reduced, :]
        row += reduced - i
    phi[row : row + 1, :] = inputs[...]
    phi[row + 1 : row + 2, :] = jnp.ones((1, count), jnp.float32)

    s = states[...]
    extra = jnp.concatenate([s * s * (0.5**0.5), jnp.broadcast_to(inputs[...], (8, count)) * (8.0**-0.5)], 0)
    inner = exact(s.T, s)
    system[...] = (inner + 0.5 * inner * inner + exact(extra.T, extra) + 1.0) * (1.0 / count)
    diagonal = eye_mask(count)
    a = system[...] + jnp.where(diagonal, penalty, 0.0)
    system[...] = a

    high = jnp.max(jnp.sum(jnp.abs(a), axis=0, keepdims=True)) / penalty
    delta = (high - 1.0) / (high + 1.0)
    alpha = 2.0 / ((1.0 + high) * penalty)
    c = 2.0 / (2.0 - delta * delta)
    inverse[...] = (c * alpha) * (jnp.where(diagonal, 2.0, 0.0) - alpha * a)
    delta = delta * delta / (2.0 - delta * delta)

    def coarse(state):
        step, delta = state
        x = inverse[...].astype(jnp.bfloat16)
        shifted[...] = fast(system[...], x)
        c = 2.0 / (2.0 - delta * delta)
        inverse[...] = c * (2.0 * inverse[...] - fast(x, shifted[...]))
        return step + 1, delta * delta / (2.0 - delta * delta)

    lax.while_loop(lambda state: (state[1] > 0.1) & (state[0] < 12), coarse, (0, delta))

    def polish(state):
        step, _ = state
        x = inverse[...]
        gap = jnp.where(eye_mask(count), 1.0, 0.0) - triple(system[...], x)
        shifted[...] = gap
        worst = jnp.sum(jnp.sum(gap * gap, axis=0, keepdims=True))
        inverse[...] = inverse[...] + fast(inverse[...], shifted[...])
        return step + 1, worst

    _, worst = lax.while_loop(
        lambda state: jnp.logical_not(state[1] < 0.02) & (state[0] < 6), polish, (0, jnp.float32(1e9))
    )

    @pl.when(jnp.logical_not(worst < 0.02))
    def _():
        invert_by_pivots(system, inverse)

    y = refined_solve(targets[...] * (1.0 / count), system[...], inverse[...])
    local[...] = exact(y, phi[...], NT)


def second_step(local, mean, system, inverse, phi):
    c = 2.0 * mean - local
    z = exact(c, phi) * (1.0 / (phi.shape[1] * penalty))
    return 2.0 * mean - exact(refined_solve(z, system, inverse), phi, NT)


def second_kernel(local, mean, system, inverse, phi, out):
    out[...] = second_step(local[...], mean[...], system[...], inverse[...], phi[...])


PARAMS = dict(vmem_limit_bytes=60 * 2**20)


def first_call(states, inputs, targets, width):
    count = states.shape[1]
    vmem = pl.BlockSpec(memory_space=pltpu.VMEM)
    square = jax.ShapeDtypeStruct((count, count), jnp.float32)
    return pl.pallas_call(
        first_kernel,
        out_shape=(
            jax.ShapeDtypeStruct((targets.shape[0], width), jnp.float32),
            square,
            square,
            jax.ShapeDtypeStruct((width, count), jnp.float32),
        ),
        in_specs=[vmem] * 3,
        out_specs=(vmem,) * 4,
        scratch_shapes=[pltpu.VMEM((count, count), jnp.float32)],
        compiler_params=pltpu.CompilerParams(**PARAMS),
        name="local_first",
    )(states, inputs, targets)


def shards(states, inputs, targets):
    reduced = states.shape[0]
    feat_count = lax.axis_size("feat")
    slab_count = lax.axis_size("slab")
    half = reduced // feat_count
    width = reduced + reduced * (reduced + 1) // 2 + 2
    packed = jnp.concatenate([states, targets, inputs[None]], 0)
    full = lax.all_gather(packed, "feat", axis=1, tiled=True)
    first_row = lax.axis_index("feat") * half
    picked = lax.dynamic_slice_in_dim(full[reduced : 2 * reduced], first_row, half, 0)
    local, system, inverse, phi = first_call(full[:reduced], full[2 * reduced :], picked, width)
    mean = lax.psum(local, "slab") / slab_count
    vmem = pl.BlockSpec(memory_space=pltpu.VMEM)
    after = pl.pallas_call(
        second_kernel,
        out_shape=jax.ShapeDtypeStruct(local.shape, jnp.float32),
        in_specs=[vmem] * 5,
        out_specs=vmem,
        compiler_params=pltpu.CompilerParams(**PARAMS),
        name="local_second",
    )(local, mean, system, inverse, phi)
    last = lax.psum(after, "slab") / slab_count
    duals = (local - mean) + (after - last)
    sums = jnp.stack(
        [
            jnp.sum(jnp.square(local - mean)),
            jnp.sum(jnp.square(after - last)),
            penalty * penalty * jnp.sum(jnp.square(mean)),
            penalty * penalty * jnp.sum(jnp.square(last - mean)),
        ]
    )
    history = lax.psum(sums, ("slab", "feat")).reshape(2, 2)
    residual_history = jnp.sqrt(history / (slab_count * reduced * width))
    return (after[None], duals[None], last, residual_history)


def solution(mesh):
    in_specs = (P(None, ("slab", "feat")), P(("slab", "feat")), P(None, ("slab", "feat")))
    out_specs = (P("slab", "feat", None), P("slab", "feat", None), P("feat", None), P())
    return jax.shard_map(shards, mesh=mesh, in_specs=in_specs, out_specs=out_specs, check_vma=False)
```

time: 600 us -> 300 us (0.50); the launches traced: 593 us -> 299 us
  other arithmetic: 236 us -> 7.56 us
  local copies, waits for them, and re-layouts: 42.8 us -> 4.81 us
  matrix products: 36.1 us -> 0 us
  Pallas kernels: 0 us -> 20.1 us
  between operations: 20.1 us -> 14.1 us
    another operation x36 -> x1, other arithmetic: 221 us -> 2.62 us  [shards(): jnp.stack([jnp.sum(jnp.square(local - mean)), jnp.sum(jnp.square(after -...]
    another operation x64 -> x0, matrix products: 25.2 us -> none  [the longest x52 13.1 us: solve_rows(): return jax.scipy.linalg.cho_solve((factor, True), right_side.T).T]
    pallas_call x0 -> x2, Pallas kernels: none -> 20.1 us  [the longest x1 12.7 us: first_call(): pl.pallas_call(first_kernel, out_shape=(jax.ShapeDtypeStruct((targets.sha...]
    another operation x34 -> x0, local copies, waits for them, and re-layouts: 20.1 us -> none  [the longest x26 18.6 us: solve_rows(): return jax.scipy.linalg.cho_solve((factor, True), right_side.T).T]
    concatenate x1 -> x0, local copies, waits for them, and re-layouts: 11.9 us -> none  [features(): return jnp.concatenate(blocks, 0)]
    dot_general x2 -> x0, matrix products: 10.9 us -> none  [product(): jnp.dot(left, right, precision=lax.Precision.HIGHEST, preferred_element_t...]
    mul x40 -> x0, other arithmetic: 7.61 us -> none  [features(): blocks.append(states[column:column + 1] * states[column:])]
  transfers between devices with their start and end apart: 2 -> 2, of which waited for: 2 -> 2; matrix products, arithmetic and copies ran while one was open for 0% -> 1% of each run, Pallas kernels for 0% -> 0%
where the time goes in v1:
time: 300 us; the launch traced here: 299 us
  waiting for transfers between devices  210 us (70%)
  blocking collectives  42.3 us (14%)
  Pallas kernels  20.1 us (7%)
  between operations  14.1 us (5%)
  other arithmetic  7.56 us (3%)
  local copies, waits for them, and re-layouts  4.81 us (2%)
    psum x1, waiting for transfers between devices, shards(): mean = lax.psum(local, 'slab') / slab_count  107 us
    psum x1, waiting for transfers between devices, shards(): last = lax.psum(after, 'slab') / slab_count  103 us
    psum x1, blocking collectives, shards(): history = lax.psum(sums, ('slab', 'feat')).reshape(2, 2)  40.2 us
    pallas_call x1, Pallas kernels, first_call(): pl.pallas_call(first_kernel, out_shape=(jax.ShapeDtypeStruct((targets.sha...  12.7 us
    pallas_call x1, Pallas kernels, shards(): pl.pallas_call(second_kernel, out_shape=jax.ShapeDtypeStruct(local.shape,...  7.43 us
  transfers between devices with their start and end apart: 2, of which 2 were waited for; matrix products, arithmetic and copies ran while one was open for 1% of the time, Pallas kernels for 0%

profile of v1, /device:TPU:0, one launch (start us, length us, event | category | flops | bytes accessed | tf_op | source)
XLA Modules:
  0.0 299.2 jit_solution(8656424180440508788)
XLA Ops:
  7.2 0.0 all-reduce.3.cloned.1.call-start
  7.2 0.8 pad_maximum_fusion
  8.0 2.1 all_gather.3
  10.1 0.6 slice.13.inputs
  10.7 0.6 fusion
  11.3 0.6 constant_dynamic-slice_fusion.targets
  11.9 12.7 %local_first.1 = (f32[20,862]{1,0:T(8,128)}, f32[512,512]{1,0:T(8,128)}, f32[512,512]{1,0:T(8,128)}, f32[862,512]{1,0:T(8,128)}) custom-call(f32[40,512]{1,0:T(8,128)} %get-tuple-element.22.states, f32[1,512]{1,0:T(1,128)} %slice.13.inputs, f32[20,512]{1,0:T(8,128)} %constant_dynamic-slice_fusion.targets), custom_call_target="tpu_custom_call" | custom-call | tf_op jit(solution)/shard_map/local_first/pallas_call | solution.py:143
  24.6 0.0 all-reduce.3.cloned.1.call-update
  24.7 0.0 all-reduce.5.cloned.1.call-start
  24.7 107.2 %all-reduce.3.cloned.1.call-done = f32[20,862]{1,0:T(8,128)} async-done(((f32[20,862]{1,0:T(8,128)}), f32[20,862]{1,0:T(8,128)}) %all-reduce.3.cloned.1.call-update) | async-done | bytes 68976 | tf_op jit(solution)/shard_map/psum | solution.py:170
  131.9 1.5 broadcast_multiply_fusion.1.mean
  133.4 0.0 copy-start
  133.4 0.0 copy-start.1
  133.4 7.4 %local_second.1 = f32[20,862]{1,0:T(8,128)} custom-call(f32[20,862]{1,0:T(8,128)} %get-tuple-element.8.local, f32[20,862]{1,0:T(8,128)} %broadcast_multiply_fusion.1.mean, f32[512,512]{1,0:T(8,128)} %get-tuple-element.9.system, f32[512,512]{1,0:T(8,128)} %get-tuple-element.10.inverse, f32[862,512]{1,0:T(8,128)} %get-tuple-element.11.phi), custom_call_target="tpu_custom_call" | custom-call | tf_op jit(solution)/shard_map/local_second/pallas_call | solution.py:172
  140.9 0.0 all-reduce.5.cloned.1.call-update
  140.9 1.6 copy.7
  142.5 103.0 %all-reduce.5.cloned.1.call-done = f32[20,862]{1,0:T(8,128)} async-done(((f32[20,862]{1,0:T(8,128)}), f32[20,862]{1,0:T(8,128)}) %all-reduce.5.cloned.1.call-update) | async-done | bytes 68976 | tf_op jit(solution)/shard_map/psum | solution.py:180
  245.5 0.0 copy-done
  245.5 0.0 copy-done.1
  245.5 1.7 multiply_reduce_fusion.3
  247.2 0.0 copy-start.2
  247.2 2.6 pad_maximum_fusion.1
  249.8 0.9 add_bitcast_fusion
  250.7 0.7 copy.8
  251.5 40.2 %psum.23 = f32[4]{0:T(128)S(1)} all-reduce(f32[4]{0:T(128)S(1)} %pad_maximum_fusion.1), channel_id=1, replica_groups=mesh['slab'=16,'feat'=2] {'slab','feat'}, use_global_device_ids=true, to_apply=%region_6.0 | all-reduce | flops 4 | bytes 32 | tf_op jit(solution)/shard_map/psum | solution.py:190
  291.7 0.7 sqrt.7
  292.4 0.0 copy-done.2
  (1 shorter events, 0.0 us)
Async XLA Ops:
  7.2 124.7 %all-reduce.3.cloned.1.call-start = ((), (), s32[]{:S(2)}) async-start(), calls=%async_computation | async-start | bytes 172032 | tf_op jit(solution)/shard_map/psum | solution.py:170
  24.7 220.9 %all-reduce.5.cloned.1.call-start = ((), (), s32[]{:S(2)}) async-start(), calls=%async_computation.1 | async-start | bytes 172032 | tf_op jit(solution)/shard_map/psum | solution.py:180
  133.4 112.1 %copy-start = (f32[20,862]{1,0:T(8,128)S(1)}, f32[20,862]{1,0:T(8,128)}, u32[]{:S(2)}) copy-start(f32[20,862]{1,0:T(8,128)} %get-tuple-element.8.local) | copy-start | bytes 206884
  133.4 112.1 %copy-start.1 = (f32[20,862]{1,0:T(8,128)S(1)}, f32[20,862]{1,0:T(8,128)}, u32[]{:S(2)}) copy-start(f32[20,862]{1,0:T(8,128)} %all-reduce.3.cloned.1.call-done) | copy-start | bytes 206884
  247.2 45.1 %copy-start.2 = (f32[20,862]{1,0:T(8,128)}, f32[20,862]{1,0:T(8,128)S(1)}, u32[]{:S(2)}) copy-start(f32[20,862]{1,0:T(8,128)S(1)} %get-tuple-element.20) | copy-start | bytes 206884
Sparse Core Ops, SparseCore 0:
  24.8 107.0 all-reduce.2
  141.0 104.4 all-reduce.4

commit v2 on v1

v2 whole, which is shorter than its diff:
```python
import functools

import jax
import jax.numpy as jnp
from jax import lax
from jax.experimental import pallas as pl
from jax.experimental.pallas import tpu as pltpu
from jax.sharding import PartitionSpec as P

penalty = 1.0
NN = (((1,), (0,)), ((), ()))
NT = (((1,), (1,)), ((), ()))


def exact(left, right, dims=NN):
    return lax.dot_general(left, right, dims, precision=lax.Precision.HIGHEST, preferred_element_type=jnp.float32)


def fast(left, right, dims=NN):
    return lax.dot_general(
        left.astype(jnp.bfloat16), right.astype(jnp.bfloat16), dims, preferred_element_type=jnp.float32
    )


def split(value):
    high = value.astype(jnp.bfloat16)
    return high, (value - high.astype(jnp.float32)).astype(jnp.bfloat16)


def triple(left, right):
    lh, ll = split(left)
    rh, rl = split(right)
    return fast(lh, rh) + (fast(lh, rl) + fast(ll, rh))


def eye_mask(size):
    return lax.broadcasted_iota(jnp.int32, (size, size), 0) == lax.broadcasted_iota(jnp.int32, (size, size), 1)


def refined_solve(right_side, system, inverse):
    answer = fast(right_side, inverse)
    for _ in range(3):
        answer = answer + fast(right_side - exact(answer, system), inverse)
    return answer


def invert_by_pivots(source, target):
    size = source.shape[0]
    target[...] = source[...]
    sub = lax.broadcasted_iota(jnp.int32, (size, 1), 0)
    lane = lax.broadcasted_iota(jnp.int32, (1, size), 1)

    def step(k, carry):
        row = target[pl.ds(k, 1), :]
        here = lane == k
        pivot = jnp.sum(jnp.where(here, row, 0.0), axis=1, keepdims=True)
        scaled = jnp.where(here, 1.0, row) / pivot
        whole = target[...]
        column = jnp.sum(jnp.where(here, whole, 0.0), axis=1, keepdims=True)
        column = jnp.where(sub == k, -1.0, column)
        kept = jnp.where(here | (sub == k), 0.0, whole)
        target[...] = kept - column * scaled
        return carry

    lax.fori_loop(0, size, step, 0)


def first_kernel(packed, local, tiles, system, inverse, phi, shifted, wanted, *, reduced, feats):
    count = packed.shape[1]
    half = reduced // feats
    row = reduced
    phi[0:reduced, :] = packed[0:reduced, :]
    for i in range(reduced):
        phi[row : row + reduced - i, :] = packed[i : i + 1, :] * packed[i:reduced, :]
        row += reduced - i
    signal = packed[2 * reduced : 2 * reduced + 1, :]
    phi[row : row + 1, :] = signal
    phi[row + 1 : row + 2, :] = jnp.ones((1, count), jnp.float32)
    if row + 2 < phi.shape[0]:
        phi[row + 2 :, :] = jnp.zeros((phi.shape[0] - row - 2, count), jnp.float32)
    wanted[...] = jnp.zeros(wanted.shape, jnp.float32)
    me = lax.axis_index("feat")
    for f in range(feats):

        @pl.when(me == f)
        def _():
            wanted[0:half, :] = packed[reduced + f * half : reduced + (f + 1) * half, :]

    s = packed[0:reduced, :]
    extra = jnp.concatenate([s * s * (0.5**0.5), jnp.broadcast_to(signal, (8, count)) * (8.0**-0.5)], 0)
    inner = exact(s.T, s)
    diagonal = eye_mask(count)
    a = (inner + 0.5 * inner * inner + exact(extra.T, extra) + 1.0) * (1.0 / count)
    a = a + jnp.where(diagonal, penalty, 0.0)
    system[...] = a

    high = jnp.max(jnp.sum(jnp.abs(a), axis=0, keepdims=True)) / penalty
    delta = (high - 1.0) / (high + 1.0)
    alpha = 2.0 / ((1.0 + high) * penalty)
    c = 2.0 / (2.0 - delta * delta)
    inverse[...] = (c * alpha) * (jnp.where(diagonal, 2.0, 0.0) - alpha * a)
    delta = delta * delta / (2.0 - delta * delta)

    def coarse(state):
        step, delta = state
        x = inverse[...].astype(jnp.bfloat16)
        shifted[...] = fast(system[...], x)
        c = 2.0 / (2.0 - delta * delta)
        inverse[...] = c * (2.0 * inverse[...] - fast(x, shifted[...]))
        return step + 1, delta * delta / (2.0 - delta * delta)

    lax.while_loop(lambda state: (state[1] > 0.1) & (state[0] < 12), coarse, (0, delta))

    def polish(state):
        step, _ = state
        x = inverse[...]
        gap = jnp.where(eye_mask(count), 1.0, 0.0) - triple(system[...], x)
        shifted[...] = gap
        worst = jnp.sum(jnp.sum(gap * gap, axis=0, keepdims=True))
        inverse[...] = inverse[...] + fast(inverse[...], shifted[...])
        return step + 1, worst

    _, worst = lax.while_loop(
        lambda state: jnp.logical_not(state[1] < 0.02) & (state[0] < 6), polish, (0, jnp.float32(1e9))
    )

    @pl.when(jnp.logical_not(worst < 0.02))
    def _():
        invert_by_pivots(system, inverse)

    y = refined_solve(wanted[...] * (1.0 / count), system[...], inverse[...])
    result = exact(y, phi[...], NT)
    local[...] = result
    to_tiles(result, tiles)


def to_tiles(value, tiles):
    rows, columns = value.shape
    spot = 0
    for c in range(0, columns, 128):
        for r in range(0, rows, 8):
            tiles[spot] = value[r : r + 8, c : c + 128]
            spot += 1
    for rest in range(spot, tiles.shape[0]):
        tiles[rest] = jnp.zeros((8, 128), jnp.float32)


def from_tiles(tile, rows, columns):
    high = rows // 8
    strips = []
    for c in range(columns // 128):
        strips.append(jnp.concatenate([tile(c * high + r) for r in range(high)], 0))
    return jnp.concatenate(strips, 1)


def total(value):
    flat = value.reshape(-1, 8, 128).sum(0)
    return jnp.sum(jnp.sum(flat, axis=1, keepdims=True), axis=0, keepdims=True)


def second_kernel(
    local, tiles, system, inverse, phi, after, duals, last, history,
    received, gathered, received2, gathered2, foreign, tiles2, stats,
    scatter_send, scatter_recv, gather_send, gather_recv,
    scatter_send2, scatter_recv2, gather_send2, gather_recv2, foreign_send, foreign_recv,
    *, reduced, width,
):
    slabs = lax.axis_size("slab")
    feats = lax.axis_size("feat")
    me = lax.axis_index("slab")
    core = lax.axis_index("feat")
    owners, extended = gathered2.shape[0], gathered2.shape[1]
    chunk = extended - 1
    rows, columns = local.shape
    half = reduced // feats

    def peer(d):
        return lax.rem(me + d, slabs)

    def feat_of(f):
        return lax.rem(core + f, feats)

    def copy(source, target, send, recv, slab, feat):
        return pltpu.make_async_remote_copy(
            src_ref=source, dst_ref=target, send_sem=send, recv_sem=recv,
            device_id={"slab": slab, "feat": feat}, device_id_type=pl.DeviceIdType.MESH,
        )

    barrier = pltpu.get_barrier_semaphore()
    for f in range(feats):

        def greet(d, carry, f=f):
            pl.semaphore_signal(
                barrier, inc=1, device_id={"slab": peer(d), "feat": feat_of(f)},
                device_id_type=pl.DeviceIdType.MESH,
            )
            return carry

        lax.fori_loop(1 if f == 0 else 0, slabs, greet, 0)
    pl.semaphore_wait(barrier, slabs * feats - 1)

    def each(first, stop, body):
        def step(d, carry):
            body(d)
            return carry

        lax.fori_loop(first, stop, step, 0)

    def scatter(source, landing, send, recv):
        def piece(d):
            owner = peer(d)
            return copy(source.at[pl.ds(owner * chunk, chunk)], landing.at[d], send.at[d], recv.at[d], owner, core)

        def start(d):
            @pl.when(peer(d) < owners)
            def _():
                piece(d).start()

        def finish(d):
            @pl.when(peer(d) < owners)
            def _():
                piece(d).wait_send()

        each(1, slabs, start)
        return finish

    def arrivals(source, landing, send, recv):
        def wait(d):
            copy(source.at[pl.ds(0, chunk)], landing.at[d], send.at[d], recv.at[d], me, core).wait_recv()

        each(1, slabs, wait)

    def spread(buffer, send, recv):
        def piece(d):
            return copy(buffer.at[me], buffer.at[me], send.at[d], recv.at[me], peer(d), core)

        each(1, slabs, lambda d: piece(d).start())
        return lambda d: piece(d).wait_send()

    def collected(buffer, send, recv):
        def wait(o):
            @pl.when(o != me)
            def _():
                copy(buffer.at[o], buffer.at[o], send.at[0], recv.at[o], me, core).wait_recv()

        each(0, owners, wait)

    end1 = scatter(tiles, received, scatter_send, scatter_recv)

    @pl.when(me < owners)
    def _():
        arrivals(tiles, received, scatter_send, scatter_recv)
        mine = tiles[pl.ds(me * chunk, chunk)]
        others = received[1:slabs]
        mean = (mine + others.sum(0)) * (1.0 / slabs)
        gathered[me] = mean
        spread(gathered, gather_send, gather_recv)
        primal = total(jnp.square(mine - mean)) + total(jnp.square(others - mean[None]))
        stats[0] = jnp.broadcast_to(primal, (8, 128))
        stats[1] = jnp.broadcast_to((slabs * penalty * penalty) * total(jnp.square(mean)), (8, 128))

    collected(gathered, gather_send, gather_recv)
    mean = from_tiles(lambda t: gathered[t // chunk, t % chunk], rows, columns)
    first = local[...]
    c = 2.0 * mean - first
    z = exact(c, phi[...]) * (1.0 / (phi.shape[1] * penalty))
    result = 2.0 * mean - exact(refined_solve(z, system[...], inverse[...]), phi[...], NT)
    to_tiles(result, tiles2)
    end2 = scatter(tiles2, received2, scatter_send2, scatter_recv2)
    after[...] = result[:half, :width]

    @pl.when(me < owners)
    def _():
        arrivals(tiles2, received2, scatter_send2, scatter_recv2)
        mine = tiles2[pl.ds(me * chunk, chunk)]
        others = received2[1:slabs]
        old = gathered[me]
        new = (mine + others.sum(0)) * (1.0 / slabs)
        primal = total(jnp.square(mine - new)) + total(jnp.square(others - new[None]))
        dual = (slabs * penalty * penalty) * total(jnp.square(new - old))
        sub = lax.broadcasted_iota(jnp.int32, (8, 128), 0)
        lane = lax.broadcasted_iota(jnp.int32, (8, 128), 1)
        top = jnp.where(lane == 0, stats[0], jnp.broadcast_to(primal, (8, 128)))
        low = jnp.where(lane == 0, stats[1], jnp.broadcast_to(dual, (8, 128)))
        gathered2[me, 0:chunk] = new
        gathered2[me, chunk] = jnp.where(sub == 0, top, low)
        spread(gathered2, gather_send2, gather_recv2)
        for f in range(1, feats):

            def outward(d, f=f):
                copy(
                    gathered2.at[me, chunk], foreign.at[f - 1, me], foreign_send.at[f - 1, d],
                    foreign_recv.at[f - 1, me], peer(d), feat_of(f),
                ).start()

            each(0, slabs, outward)

    collected(gathered2, gather_send2, gather_recv2)
    new = from_tiles(lambda t: gathered2[t // chunk, t % chunk], rows, columns)
    last[...] = new[:half, :width]
    change = (first - mean) + (result - new)
    duals[...] = change[:half, :width]
    sums = gathered2[0, chunk]
    for o in range(1, owners):
        sums = sums + gathered2[o, chunk]
    for f in range(1, feats):

        def inward(o, f=f):
            copy(
                gathered2.at[0, chunk], foreign.at[f - 1, o], foreign_send.at[f - 1, 0],
                foreign_recv.at[f - 1, o], me, core,
            ).wait_recv()

        each(0, owners, inward)
        for o in range(owners):
            sums = sums + foreign[f - 1, o]
    history[...] = jnp.sqrt(sums * (1.0 / (slabs * reduced * width)))[0:2, 0:2]

    each(1, slabs, end1)
    each(1, slabs, end2)

    @pl.when(me < owners)
    def _():
        def leave(d):
            copy(gathered.at[me], gathered.at[me], gather_send.at[d], gather_recv.at[me], peer(d), core).wait_send()
            copy(
                gathered2.at[me], gathered2.at[me], gather_send2.at[d], gather_recv2.at[me], peer(d), core
            ).wait_send()

        each(1, slabs, leave)
        for f in range(1, feats):

            def depart(d, f=f):
                copy(
                    gathered2.at[me, chunk], foreign.at[f - 1, me], foreign_send.at[f - 1, d],
                    foreign_recv.at[f - 1, me], peer(d), feat_of(f),
                ).wait_send()

            each(0, slabs, depart)


LIMIT = 60 * 2**20


def up(value, step):
    return -(-value // step) * step


def shards(states, inputs, targets):
    reduced = states.shape[0]
    feats = lax.axis_size("feat")
    slabs = lax.axis_size("slab")
    half = reduced // feats
    width = reduced + reduced * (reduced + 1) // 2 + 2
    count = states.shape[1] * feats
    rows, columns = up(half, 8), up(width, 128)
    pieces = (rows // 8) * (columns // 128)
    chunk = -(-pieces // slabs)
    owners = -(-pieces // chunk)
    f32 = jnp.float32
    packed = lax.all_gather(jnp.concatenate([states, targets, inputs[None]], 0), "feat", axis=1, tiled=True)
    vmem = pl.BlockSpec(memory_space=pltpu.VMEM)
    square = jax.ShapeDtypeStruct((count, count), f32)
    local, tiles, system, inverse, phi = pl.pallas_call(
        functools.partial(first_kernel, reduced=reduced, feats=feats),
        out_shape=(
            jax.ShapeDtypeStruct((rows, columns), f32),
            jax.ShapeDtypeStruct((owners * chunk, 8, 128), f32),
            square,
            square,
            jax.ShapeDtypeStruct((columns, count), f32),
        ),
        in_specs=[vmem],
        out_specs=(vmem,) * 5,
        scratch_shapes=[pltpu.VMEM((count, count), f32), pltpu.VMEM((rows, count), f32)],
        compiler_params=pltpu.CompilerParams(vmem_limit_bytes=LIMIT),
        name="local_first",
    )(packed)
    shard = jax.ShapeDtypeStruct((half, width), f32)
    dma = pltpu.SemaphoreType.DMA
    after, duals, last, history = pl.pallas_call(
        functools.partial(second_kernel, reduced=reduced, width=width),
        out_shape=(shard, shard, shard, jax.ShapeDtypeStruct((2, 2), f32)),
        in_specs=[vmem] * 5,
        out_specs=(vmem,) * 4,
        scratch_shapes=[
            pltpu.VMEM((slabs, chunk, 8, 128), f32),
            pltpu.VMEM((owners, chunk, 8, 128), f32),
            pltpu.VMEM((slabs, chunk, 8, 128), f32),
            pltpu.VMEM((owners, chunk + 1, 8, 128), f32),
            pltpu.VMEM((max(feats - 1, 1), owners, 8, 128), f32),
            pltpu.VMEM((owners * chunk, 8, 128), f32),
            pltpu.VMEM((2, 8, 128), f32),
            dma((slabs,)), dma((slabs,)), dma((slabs,)), dma((owners,)),
            dma((slabs,)), dma((slabs,)), dma((slabs,)), dma((owners,)),
            dma((max(feats - 1, 1), slabs)), dma((max(feats - 1, 1), owners)),
        ],
        compiler_params=pltpu.CompilerParams(vmem_limit_bytes=LIMIT, collective_id=0, has_side_effects=True),
        name="second_and_averages",
    )(local, tiles, system, inverse, phi)
    return (after[None], duals[None], last, history)


def solution(mesh):
    in_specs = (P(None, ("slab", "feat")), P(("slab", "feat")), P(None, ("slab", "feat")))
    out_specs = (P("slab", "feat", None), P("slab", "feat", None), P("feat", None), P())
    return jax.shard_map(shards, mesh=mesh, in_specs=in_specs, out_specs=out_specs, check_vma=False)
```

time: 300 us -> 58.5 us (0.20)
  waiting for transfers between devices: 210 us -> 0 us
  blocking collectives: 42.3 us -> 2.19 us
  Pallas kernels: 20.1 us -> 48.6 us
  between operations: 14.1 us -> 0.64 us
  other arithmetic: 7.56 us -> 0.82 us
    psum x2 -> x0, waiting for transfers between devices: 210 us -> none  [the longest x1 107 us: shards(): mean = lax.psum(local, 'slab') / slab_count]
    psum x1 -> x0, blocking collectives: 40.2 us -> none  [shards(): history = lax.psum(sums, ('slab', 'feat')).reshape(2, 2)]
    pallas_call x2, Pallas kernels: 20.1 us -> 48.6 us  [the longest x1 34.6 us: shards(): pl.pallas_call(functools.partial(second_kernel, reduced=reduced, width=wi...]
    unnamed x8 -> x4, local copies, waits for them, and re-layouts: 2.31 us -> 5.94 us
  transfers between devices with their start and end apart: 2 -> 0, of which waited for: 2 -> 0; matrix products, arithmetic and copies ran while one was open for 1% -> 0% of each run, Pallas kernels for 0% -> 0%
where the time goes in v2:
time: 58.5 us; the launch traced here: 58.2 us
  Pallas kernels  48.6 us (83%)
  local copies, waits for them, and re-layouts  5.94 us (10%)
  blocking collectives  2.19 us (4%)
  other arithmetic  0.82 us (1%)
  between operations  0.64 us (1%)
    pallas_call x1, Pallas kernels, shards(): pl.pallas_call(functools.partial(second_kernel, reduced=reduced, width=wi...  34.6 us
    pallas_call x1, Pallas kernels, shards(): pl.pallas_call(functools.partial(first_kernel, reduced=reduced, feats=fea...  14 us
    unnamed x4, local copies, waits for them, and re-layouts  5.94 us
    all_gather x1, blocking collectives, shards(): lax.all_gather(jnp.concatenate([states, targets, inputs[None]], 0), 'feat...  2.19 us

profile of v2, /device:TPU:0, one launch (start us, length us, event | category | flops | bytes accessed | tf_op | source)
XLA Modules:
  0.0 58.2 jit_solution(1448275100063477205)
XLA Ops:
  0.6 0.8 %pad_maximum_fusion = f32[81,256]{1,0:T(8,128)S(1)} fusion(f32[1,256]{1,0:T(1,128)} %bitcast.5, f32[40,256]{1,0:T(8,128)} %param.5, f32[40,256]{1,0:T(8,128)} %param.3), kind=kLoop, calls=%fused_computation | loop fusion | flops 41472 | bytes 165888 | tf_op jit(solution)/shard_map/concatenate | solution.py:361
  1.5 2.2 %all_gather.3.packed = f32[81,512]{1,0:T(8,128)} all-gather(f32[81,256]{1,0:T(8,128)S(1)} %pad_maximum_fusion), channel_id=1, replica_groups=mesh['slab'=16,'feat'=2] {'feat'}, dimensions={1}, use_global_device_ids=true | all-gather | bytes 248832 | tf_op jit(solution)/shard_map/all_gather | solution.py:361
  3.6 14.0 %local_first.1 = (f32[24,896]{1,0:T(8,128)}, f32[22,8,128]{2,1,0:T(8,128)}, f32[512,512]{1,0:T(8,128)}, f32[512,512]{1,0:T(8,128)}, f32[896,512]{1,0:T(8,128)}) custom-call(f32[81,512]{1,0:T(8,128)} %all_gather.3.packed), custom_call_target="tpu_custom_call" | custom-call | tf_op jit(solution)/shard_map/local_first/pallas_call | solution.py:364
  17.7 34.6 %second_and_averages.1 = (f32[20,862]{1,0:T(8,128)}, f32[20,862]{1,0:T(8,128)}, f32[20,862]{1,0:T(8,128)}, f32[2,2]{1,0:T(2,128)}) custom-call(f32[24,896]{1,0:T(8,128)} %get-tuple-element.13.local, f32[22,8,128]{2,1,0:T(8,128)} %get-tuple-element.14.tiles, f32[512,512]{1,0:T(8,128)} %get-tuple-element.15.system, f32[512,512]{1,0:T(8,128)} %get-tuple-element.16.inverse, ...), custom_call_target="tpu_custom_call" | custom-call | tf_op jit(solution)/shard_map/second_and_averages/pallas_call | solution.py:381
  52.2 1.6 %copy.7 = f32[1,20,862]{2,0,1:T(1,128)} copy(f32[1,20,862]{2,1,0:T(8,128)} %bitcast.4) | data formatting | bytes 137920
  53.8 1.6 %copy.8 = f32[1,20,862]{2,0,1:T(1,128)} copy(f32[1,20,862]{2,1,0:T(8,128)} %bitcast.3) | data formatting | bytes 137920
  55.4 1.5 %copy.11 = f32[20,862]{1,0:T(8,128)} copy(f32[20,862]{1,0:T(8,128)} %get-tuple-element.32) | data formatting | bytes 137920
  57.0 1.2 %copy.12 = f32[2,2]{1,0:T(2,128)} copy(f32[2,2]{1,0:T(2,128)} %get-tuple-element.33) | data formatting | bytes 32

commit v3 on v2

--- a/solution.py
+++ b/solution.py
@@ -172,7 +172,6 @@
     owners, extended = gathered2.shape[0], gathered2.shape[1]
     chunk = extended - 1
     rows, columns = local.shape
-    half = reduced // feats
 
     def peer(d):
         return lax.rem(me + d, slabs)
@@ -186,25 +185,29 @@
             device_id={"slab": slab, "feat": feat}, device_id_type=pl.DeviceIdType.MESH,
         )
 
+    def each(first, stop, body):
+        if stop - first <= 16:
+            for d in range(first, stop):
+                body(d)
+            return
+
+        def step(d, carry):
+            body(d)
+            return carry
+
+        lax.fori_loop(first, stop, step, 0)
+
     barrier = pltpu.get_barrier_semaphore()
     for f in range(feats):
 
-        def greet(d, carry, f=f):
+        def greet(d, f=f):
             pl.semaphore_signal(
                 barrier, inc=1, device_id={"slab": peer(d), "feat": feat_of(f)},
                 device_id_type=pl.DeviceIdType.MESH,
             )
-            return carry
-
-        lax.fori_loop(1 if f == 0 else 0, slabs, greet, 0)
+
+        each(1 if f == 0 else 0, slabs, greet)
     pl.semaphore_wait(barrier, slabs * feats - 1)
-
-    def each(first, stop, body):
-        def step(d, carry):
-            body(d)
-            return carry
-
-        lax.fori_loop(first, stop, step, 0)
 
     def scatter(source, landing, send, recv):
         def piece(d):
@@ -267,7 +270,7 @@
     result = 2.0 * mean - exact(refined_solve(z, system[...], inverse[...]), phi[...], NT)
     to_tiles(result, tiles2)
     end2 = scatter(tiles2, received2, scatter_send2, scatter_recv2)
-    after[...] = result[:half, :width]
+    after[...] = result
 
     @pl.when(me < owners)
     def _():
@@ -297,9 +300,9 @@
 
     collected(gathered2, gather_send2, gather_recv2)
     new = from_tiles(lambda t: gathered2[t // chunk, t % chunk], rows, columns)
-    last[...] = new[:half, :width]
+    last[...] = new
     change = (first - mean) + (result - new)
-    duals[...] = change[:half, :width]
+    duals[...] = change
     sums = gathered2[0, chunk]
     for o in range(1, owners):
         sums = sums + gathered2[o, chunk]
@@ -314,7 +317,7 @@
         each(0, owners, inward)
         for o in range(owners):
             sums = sums + foreign[f - 1, o]
-    history[...] = jnp.sqrt(sums * (1.0 / (slabs * reduced * width)))[0:2, 0:2]
+    history[...] = jnp.sqrt(sums * (1.0 / (slabs * reduced * width)))
 
     each(1, slabs, end1)
     each(1, slabs, end2)
@@ -339,7 +342,16 @@
             each(0, slabs, depart)
 
 
-LIMIT = 60 * 2**20
+def last_kernel(after, duals, last, history, out_after, out_duals, out_last, out_history):
+    half, width = out_last.shape
+    for r in range(half):
+        out_after[r] = after[r : r + 1, :width]
+        out_duals[r] = duals[r : r + 1, :width]
+    out_last[...] = last[:half, :width]
+    out_history[...] = history[0:2, 0:2]
+
+
+LIMIT = 20 * 2**20
 
 
 def up(value, step):
@@ -377,10 +389,12 @@
         name="local_first",
     )(packed)
     shard = jax.ShapeDtypeStruct((half, width), f32)
+    spread_rows = jax.ShapeDtypeStruct((half, 1, width), f32)
+    block = jax.ShapeDtypeStruct((rows, columns), f32)
     dma = pltpu.SemaphoreType.DMA
     after, duals, last, history = pl.pallas_call(
         functools.partial(second_kernel, reduced=reduced, width=width),
-        out_shape=(shard, shard, shard, jax.ShapeDtypeStruct((2, 2), f32)),
+        out_shape=(block, block, block, jax.ShapeDtypeStruct((8, 128), f32)),
         in_specs=[vmem] * 5,
         out_specs=(vmem,) * 4,
         scratch_shapes=[
@@ -398,7 +412,15 @@
         compiler_params=pltpu.CompilerParams(vmem_limit_bytes=LIMIT, collective_id=0, has_side_effects=True),
         name="second_and_averages",
     )(local, tiles, system, inverse, phi)
-    return (after[None], duals[None], last, history)
+    after, duals, last, history = pl.pallas_call(
+        last_kernel,
+        out_shape=(spread_rows, spread_rows, shard, jax.ShapeDtypeStruct((2, 2), f32)),
+        in_specs=[vmem] * 4,
+        out_specs=(vmem,) * 4,
+        compiler_params=pltpu.CompilerParams(vmem_limit_bytes=4 * 2**20),
+        name="outputs",
+    )(after, duals, last, history)
+    return (jnp.swapaxes(after, 0, 1), jnp.swapaxes(duals, 0, 1), last, history)
 
 
 def solution(mesh):

time: 58.5 us -> 48.4 us (0.83)
  local copies, waits for them, and re-layouts: 5.94 us -> 0 us
  Pallas kernels: 48.6 us -> 44.7 us
    unnamed x4 -> x0, local copies, waits for them, and re-layouts: 5.94 us -> none
    pallas_call x1, Pallas kernels: 14 us -> 11.3 us  [shards(): pl.pallas_call(functools.partial(first_kernel, reduced=reduced, feats=fea...]
    pallas_call x1, Pallas kernels: 34.6 us -> 32.6 us  [shards(): pl.pallas_call(functools.partial(second_kernel, reduced=reduced, width=wi...]
    pallas_call x0 -> x1, Pallas kernels: none -> 0.73 us  [shards(): pl.pallas_call(last_kernel, out_shape=(spread_rows, spread_rows, shard, j...]
where the time goes in v3:
time: 48.4 us; the launch traced here: 48.2 us
  Pallas kernels  44.7 us (92%)
  blocking collectives  2.06 us (4%)
  other arithmetic  0.82 us (2%)
  between operations  0.64 us (1%)
    pallas_call x1, Pallas kernels, shards(): pl.pallas_call(functools.partial(second_kernel, reduced=reduced, width=wi...  32.6 us
    pallas_call x1, Pallas kernels, shards(): pl.pallas_call(functools.partial(first_kernel, reduced=reduced, feats=fea...  11.3 us
    all_gather x1, blocking collectives, shards(): lax.all_gather(jnp.concatenate([states, targets, inputs[None]], 0), 'feat...  2.06 us

profile of v3, /device:TPU:0, one launch (start us, length us, event | category | flops | bytes accessed | tf_op | source)
XLA Modules:
  0.0 48.2 jit_solution(15114236181539258141)
XLA Ops:
  0.6 0.8 %pad_maximum_fusion = f32[81,256]{1,0:T(8,128)S(1)} fusion(f32[1,256]{1,0:T(1,128)} %bitcast.3, f32[40,256]{1,0:T(8,128)} %param.5, f32[40,256]{1,0:T(8,128)} %param.3), kind=kLoop, calls=%fused_computation | loop fusion | flops 41472 | bytes 165888 | tf_op jit(solution)/shard_map/concatenate | solution.py:373
  1.5 2.1 %all_gather.3.packed = f32[81,512]{1,0:T(8,128)S(1)} all-gather(f32[81,256]{1,0:T(8,128)S(1)} %pad_maximum_fusion), channel_id=1, replica_groups=mesh['slab'=16,'feat'=2] {'feat'}, dimensions={1}, use_global_device_ids=true | all-gather | bytes 248832 | tf_op jit(solution)/shard_map/all_gather | solution.py:373
  3.5 11.3 %local_first.1 = (f32[24,896]{1,0:T(8,128)S(1)}, f32[22,8,128]{2,1,0:T(8,128)S(1)}, f32[512,512]{1,0:T(8,128)S(1)}, f32[512,512]{1,0:T(8,128)S(1)}, f32[896,512]{1,0:T(8,128)S(1)}) custom-call(f32[81,512]{1,0:T(8,128)S(1)} %all_gather.3.packed), custom_call_target="tpu_custom_call" | custom-call | tf_op jit(solution)/shard_map/local_first/pallas_call | solution.py:376
  14.8 32.6 %second_and_averages.1 = (f32[24,896]{1,0:T(8,128)S(1)}, f32[24,896]{1,0:T(8,128)S(1)}, f32[24,896]{1,0:T(8,128)S(1)}, f32[8,128]{1,0:T(8,128)S(1)}) custom-call(f32[24,896]{1,0:T(8,128)S(1)} %get-tuple-element.17.local, f32[22,8,128]{2,1,0:T(8,128)S(1)} %get-tuple-element.18.tiles, f32[512,512]{1,0:T(8,128)S(1)} %get-tuple-element.19.system, ...), custom_call_target="tpu_custom_call" | custom-call | tf_op jit(solution)/shard_map/second_and_averages/pallas_call | solution.py:395
  47.5 0.7 %outputs.1 = (f32[20,1,862]{2,1,0:T(1,128)}, f32[20,1,862]{2,1,0:T(1,128)}, f32[20,862]{1,0:T(8,128)}, f32[2,2]{1,0:T(2,128)}) custom-call(f32[24,896]{1,0:T(8,128)S(1)} %get-tuple-element.22.after, f32[24,896]{1,0:T(8,128)S(1)} %get-tuple-element.23.duals, f32[24,896]{1,0:T(8,128)S(1)} %get-tuple-element.24.last, f32[8,128]{1,0:T(8,128)S(1)} %get-tuple-element.25.history), custom_call_target="tpu_custom_call" | custom-call | tf_op jit(solution)/shard_map/outputs/pallas_call | solution.py:415

commit v4 on v3

--- a/solution.py
+++ b/solution.py
@@ -65,7 +65,7 @@
     lax.fori_loop(0, size, step, 0)
 
 
-def first_kernel(packed, local, tiles, system, inverse, phi, shifted, wanted, *, reduced, feats):
+def build_features(packed, phi, wanted, reduced, feats):
     count = packed.shape[1]
     half = reduced // feats
     row = reduced
@@ -73,8 +73,7 @@
     for i in range(reduced):
         phi[row : row + reduced - i, :] = packed[i : i + 1, :] * packed[i:reduced, :]
         row += reduced - i
-    signal = packed[2 * reduced : 2 * reduced + 1, :]
-    phi[row : row + 1, :] = signal
+    phi[row : row + 1, :] = packed[2 * reduced : 2 * reduced + 1, :]
     phi[row + 1 : row + 2, :] = jnp.ones((1, count), jnp.float32)
     if row + 2 < phi.shape[0]:
         phi[row + 2 :, :] = jnp.zeros((phi.shape[0] - row - 2, count), jnp.float32)
@@ -86,6 +85,10 @@
         def _():
             wanted[0:half, :] = packed[reduced + f * half : reduced + (f + 1) * half, :]
 
+
+def first_kernel(packed, system, inverse, shifted, *, reduced):
+    count = packed.shape[1]
+    signal = packed[2 * reduced : 2 * reduced + 1, :]
     s = packed[0:reduced, :]
     extra = jnp.concatenate([s * s * (0.5**0.5), jnp.broadcast_to(signal, (8, count)) * (8.0**-0.5)], 0)
     inner = exact(s.T, s)
@@ -127,11 +130,6 @@
     @pl.when(jnp.logical_not(worst < 0.02))
     def _():
         invert_by_pivots(system, inverse)
-
-    y = refined_solve(wanted[...] * (1.0 / count), system[...], inverse[...])
-    result = exact(y, phi[...], NT)
-    local[...] = result
-    to_tiles(result, tiles)
 
 
 def to_tiles(value, tiles):
@@ -159,8 +157,8 @@
 
 
 def second_kernel(
-    local, tiles, system, inverse, phi, after, duals, last, history,
-    received, gathered, received2, gathered2, foreign, tiles2, stats,
+    packed, system, inverse, after, duals, last, history,
+    local, tiles, phi, wanted, better, received, gathered, received2, gathered2, foreign, tiles2, stats,
     scatter_send, scatter_recv, gather_send, gather_recv,
     scatter_send2, scatter_recv2, gather_send2, gather_recv2, foreign_send, foreign_recv,
     *, reduced, width,
@@ -207,6 +205,11 @@
             )
 
         each(1 if f == 0 else 0, slabs, greet)
+    build_features(packed, phi, wanted, reduced, feats)
+    y = refined_solve(wanted[...] * (1.0 / phi.shape[1]), system[...], inverse[...])
+    start_value = exact(y, phi[...], NT)
+    local[...] = start_value
+    to_tiles(start_value, tiles)
     pl.semaphore_wait(barrier, slabs * feats - 1)
 
     def scatter(source, landing, send, recv):
@@ -248,7 +251,12 @@
 
         each(0, owners, wait)
 
+    def polished(x):
+        gap = jnp.where(eye_mask(x.shape[0]), 1.0, 0.0) - exact(system[...], x)
+        return x + fast(x, gap)
+
     end1 = scatter(tiles, received, scatter_send, scatter_recv)
+    better[...] = polished(inverse[...])
 
     @pl.when(me < owners)
     def _():
@@ -262,12 +270,13 @@
         stats[0] = jnp.broadcast_to(primal, (8, 128))
         stats[1] = jnp.broadcast_to((slabs * penalty * penalty) * total(jnp.square(mean)), (8, 128))
 
+    better[...] = polished(better[...])
     collected(gathered, gather_send, gather_recv)
     mean = from_tiles(lambda t: gathered[t // chunk, t % chunk], rows, columns)
     first = local[...]
     c = 2.0 * mean - first
     z = exact(c, phi[...]) * (1.0 / (phi.shape[1] * penalty))
-    result = 2.0 * mean - exact(refined_solve(z, system[...], inverse[...]), phi[...], NT)
+    result = 2.0 * mean - exact(exact(z, better[...]), phi[...], NT)
     to_tiles(result, tiles2)
     end2 = scatter(tiles2, received2, scatter_send2, scatter_recv2)
     after[...] = result
@@ -373,20 +382,14 @@
     packed = lax.all_gather(jnp.concatenate([states, targets, inputs[None]], 0), "feat", axis=1, tiled=True)
     vmem = pl.BlockSpec(memory_space=pltpu.VMEM)
     square = jax.ShapeDtypeStruct((count, count), f32)
-    local, tiles, system, inverse, phi = pl.pallas_call(
-        functools.partial(first_kernel, reduced=reduced, feats=feats),
-        out_shape=(
-            jax.ShapeDtypeStruct((rows, columns), f32),
-            jax.ShapeDtypeStruct((owners * chunk, 8, 128), f32),
-            square,
-            square,
-            jax.ShapeDtypeStruct((columns, count), f32),
-        ),
+    system, inverse = pl.pallas_call(
+        functools.partial(first_kernel, reduced=reduced),
+        out_shape=(square, square),
         in_specs=[vmem],
-        out_specs=(vmem,) * 5,
-        scratch_shapes=[pltpu.VMEM((count, count), f32), pltpu.VMEM((rows, count), f32)],
+        out_specs=(vmem,) * 2,
+        scratch_shapes=[pltpu.VMEM((count, count), f32)],
         compiler_params=pltpu.CompilerParams(vmem_limit_bytes=LIMIT),
-        name="local_first",
+        name="local_inverse",
     )(packed)
     shard = jax.ShapeDtypeStruct((half, width), f32)
     spread_rows = jax.ShapeDtypeStruct((half, 1, width), f32)
@@ -395,9 +398,14 @@
     after, duals, last, history = pl.pallas_call(
         functools.partial(second_kernel, reduced=reduced, width=width),
         out_shape=(block, block, block, jax.ShapeDtypeStruct((8, 128), f32)),
-        in_specs=[vmem] * 5,
+        in_specs=[vmem] * 3,
         out_specs=(vmem,) * 4,
         scratch_shapes=[
+            pltpu.VMEM((rows, columns), f32),
+            pltpu.VMEM((owners * chunk, 8, 128), f32),
+            pltpu.VMEM((columns, count), f32),
+            pltpu.VMEM((rows, count), f32),
+            pltpu.VMEM((count, count), f32),
             pltpu.VMEM((slabs, chunk, 8, 128), f32),
             pltpu.VMEM((owners, chunk, 8, 128), f32),
             pltpu.VMEM((slabs, chunk, 8, 128), f32),
@@ -411,7 +419,7 @@
         ],
         compiler_params=pltpu.CompilerParams(vmem_limit_bytes=LIMIT, collective_id=0, has_side_effects=True),
         name="second_and_averages",
-    )(local, tiles, system, inverse, phi)
+    )(packed, system, inverse)
     after, duals, last, history = pl.pallas_call(
         last_kernel,
         out_shape=(spread_rows, spread_rows, shard, jax.ShapeDtypeStruct((2, 2), f32)),

time: 48.4 us -> 44.5 us (0.919)
  Pallas kernels: 44.7 us -> 40 us
  local copies, waits for them, and re-layouts: 0 us -> 0.67 us
    pallas_call x1, Pallas kernels: 11.3 us -> 7.37 us  [shards(): pl.pallas_call(functools.partial(first_kernel, reduced=reduced), out_shap...]
    pallas_call x1, Pallas kernels: 32.6 us -> 31.9 us  [shards(): pl.pallas_call(functools.partial(second_kernel, reduced=reduced, width=wi...]
    unnamed x0 -> x2, local copies, waits for them, and re-layouts: none -> 0.67 us
where the time goes in v4:
time: 44.5 us; the launch traced here: 44.2 us
  Pallas kernels  40 us (90%)
  blocking collectives  2.06 us (5%)
  other arithmetic  0.81 us (2%)
  local copies, waits for them, and re-layouts  0.67 us (2%)
  between operations  0.66 us (1%)
    pallas_call x1, Pallas kernels, shards(): pl.pallas_call(functools.partial(second_kernel, reduced=reduced, width=wi...  31.9 us
    pallas_call x1, Pallas kernels, shards(): pl.pallas_call(functools.partial(first_kernel, reduced=reduced), out_shap...  7.37 us
    all_gather x1, blocking collectives, shards(): lax.all_gather(jnp.concatenate([states, targets, inputs[None]], 0), 'feat...  2.06 us

profile of v4, /device:TPU:0, one launch (start us, length us, event | category | flops | bytes accessed | tf_op | source)
XLA Modules:
  0.0 44.2 jit_solution(9596675068360511245)
XLA Ops:
  0.6 0.0 copy-start
  0.6 0.7 %copy-done = f32[256]{0:T(256)S(1)} copy-done((f32[256]{0:T(256)S(1)}, f32[256]{0:T(256)}, u32[]{:S(2)}) %copy-start) | copy-done | bytes 1048
  1.3 0.8 %pad_maximum_fusion = f32[81,256]{1,0:T(8,128)S(1)} fusion(f32[1,256]{1,0:T(1,128)S(1)} %bitcast.3, f32[40,256]{1,0:T(8,128)} %param.5, f32[40,256]{1,0:T(8,128)} %param.3), kind=kLoop, calls=%fused_computation | loop fusion | flops 41472 | bytes 165888 | tf_op jit(solution)/shard_map/concatenate | solution.py:382
  2.1 2.1 %all_gather.3.packed = f32[81,512]{1,0:T(8,128)S(1)} all-gather(f32[81,256]{1,0:T(8,128)S(1)} %pad_maximum_fusion), channel_id=1, replica_groups=mesh['slab'=16,'feat'=2] {'feat'}, dimensions={1}, use_global_device_ids=true | all-gather | bytes 248832 | tf_op jit(solution)/shard_map/all_gather | solution.py:382
  4.2 7.4 %local_inverse.1 = (f32[512,512]{1,0:T(8,128)S(1)}, f32[512,512]{1,0:T(8,128)S(1)}) custom-call(f32[81,512]{1,0:T(8,128)S(1)} %all_gather.3.packed), custom_call_target="tpu_custom_call" | custom-call | tf_op jit(solution)/shard_map/local_inverse/pallas_call | solution.py:385
  11.6 31.9 %second_and_averages.1 = (f32[24,896]{1,0:T(8,128)S(1)}, f32[24,896]{1,0:T(8,128)S(1)}, f32[24,896]{1,0:T(8,128)S(1)}, f32[8,128]{1,0:T(8,128)S(1)}) custom-call(f32[81,512]{1,0:T(8,128)S(1)} %all_gather.3.packed, f32[512,512]{1,0:T(8,128)S(1)} %get-tuple-element.14.system, f32[512,512]{1,0:T(8,128)S(1)} %get-tuple-element.15.inverse), custom_call_target="tpu_custom_call" | custom-call | tf_op jit(solution)/shard_map/second_and_averages/pallas_call | solution.py:398
  43.4 0.7 %outputs.1 = (f32[20,1,862]{2,1,0:T(1,128)}, f32[20,1,862]{2,1,0:T(1,128)}, f32[20,862]{1,0:T(8,128)}, f32[2,2]{1,0:T(2,128)}) custom-call(f32[24,896]{1,0:T(8,128)S(1)} %get-tuple-element.16.after, f32[24,896]{1,0:T(8,128)S(1)} %get-tuple-element.17.duals, f32[24,896]{1,0:T(8,128)S(1)} %get-tuple-element.18.last, f32[8,128]{1,0:T(8,128)S(1)} %get-tuple-element.19.history), custom_call_target="tpu_custom_call" | custom-call | tf_op jit(solution)/shard_map/outputs/pallas_call | solution.py:423
Async XLA Ops:
  0.6 0.7 %copy-start = (f32[256]{0:T(256)S(1)}, f32[256]{0:T(256)}, u32[]{:S(2)}) copy-start(f32[256]{0:T(256)} %param.4) | copy-start | bytes 3076
